TPU v7x, 128 devices: a whole 4x4x4 slice. The times are simulated.
128 devices in a mesh: expert: 32 (over x, y, core), tensor: 4 (over z).
Axes of the slice: x: 4, y: 4, z: 4, core: 2. Of those that a mesh axis runs over, the one named last changes fastest.
Arguments:
- tokens: bfloat16 [65536, 512], P(('expert', 'tensor')), may hold values from -6 to 6
- first_gain: float32 [512], replicated, may hold values from 0.5 to 1.5
- second_gain: float32 [512], replicated, may hold values from 0.5 to 1.5
- query_weight: bfloat16 [512, 512], P(None, 'tensor'), may hold values from -0.25 to 0.25
- key_weight: bfloat16 [512, 512], P(None, 'tensor'), may hold values from -0.25 to 0.25
- value_weight: bfloat16 [512, 512], P(None, 'tensor'), may hold values from -0.25 to 0.25
- output_weight: bfloat16 [512, 512], P('tensor'), may hold values from -2 to 2
- router_weight: bfloat16 [512, 32], replicated, may hold values from -0.125 to 0.125
- expert_in: bfloat16 [32, 512, 2048], P('expert', None, 'tensor'), may hold values from -0.5 to 0.5
- expert_out: bfloat16 [32, 2048, 512], P('expert', 'tensor'), may hold values from -0.5 to 0.5
- cotangent: float32 [65536, 512], P(('expert', 'tensor')), may hold values from -6 to 6
- routes: int32 [65536, 4], P(('expert', 'tensor')), may hold values from 0 to 31, all different within a row
- priority: int32 [2048, 32], P(('expert', 'tensor')), may hold values from 0 to 31, each once within a row
- prefix_len: int32 [32], P('expert'), may hold values from 204 to 1024
Outputs:
- layer_output: bfloat16 [65536, 512], P(('expert', 'tensor'))
- tokens_grad: float32 [65536, 512], P(('expert', 'tensor'))
- first_gain_grad: float32 [512], replicated
- second_gain_grad: float32 [512], replicated
- query_grad: float32 [512, 512], P(None, 'tensor')
- key_grad: float32 [512, 512], P(None, 'tensor')
- value_grad: float32 [512, 512], P(None, 'tensor')
- output_grad: float32 [512, 512], P('tensor')
- router_grad: float32 [512, 32], replicated
- expert_in_grad: float32 [32, 512, 2048], P('expert', None, 'tensor')
- expert_out_grad: float32 [32, 2048, 512], P('expert', 'tensor')
Inputs may be any that keep to these rules, and one draw needn't show every extreme that they name: `routes`: each row names 4 different experts, and every expert is named by some row. `priority`: each row holds every number of 0 to 31 once.
All inputs are finite; a program needn't handle non-finite values.
Results may differ from a plain program's by a relative error of at most 0.028.
Values may be sent and summed in bfloat16 or wider, within the bound.
A program may use at most 128 MiB of HBM per device.

v0:
```python
import jax
import jax.numpy as jnp
from jax import lax
from jax.sharding import PartitionSpec as P

HEAD_DIM = 64
GROUP = 32
TOP = 4
EPS = 1e-05
NEG = -1e30


def norm_rows(values, gain_vec):
    center = values - jnp.mean(values, axis=-1, keepdims=True)
    spread = lax.rsqrt(jnp.mean(center * center, axis=-1, keepdims=True) + EPS)
    scaled = center * spread
    return (scaled, spread, scaled * gain_vec)


def norm_back(grad_in, scaled, spread, gain_vec):
    grad_scaled = grad_in * gain_vec
    centered = grad_scaled - jnp.mean(grad_scaled, axis=-1, keepdims=True)
    return spread * (centered - scaled * jnp.mean(grad_scaled * scaled, axis=-1, keepdims=True))


def block_scores(queries, key_rows, start_row, block_rows, prefix):
    query_blk = lax.dynamic_slice_in_dim(queries, start_row, block_rows, 0)
    scores = jnp.einsum(
        "qhd,khd->hqk", query_blk, key_rows, preferred_element_type=jnp.float32
    ) * HEAD_DIM ** (-0.5)
    row_ids = start_row + jnp.arange(block_rows, dtype=jnp.int32)
    col_ids = jnp.arange(key_rows.shape[0], dtype=jnp.int32)
    allowed = (col_ids[None, :] <= row_ids[:, None]) | (col_ids[None, :] < prefix)
    return (query_blk, jnp.where(allowed[None], scores, NEG))


def attend_forward(queries, key_rows, value_rows, prefix, block_rows):
    length = key_rows.shape[0]

    def one_block(start_row):
        query_blk, scores = block_scores(queries, key_rows, start_row, block_rows, prefix)
        row_peak = jnp.max(scores, axis=-1, keepdims=True)
        exp_scores = jnp.exp(scores - row_peak)
        exp_total = jnp.sum(exp_scores, axis=-1, keepdims=True)
        soft_rows = (exp_scores / exp_total).astype(jnp.bfloat16)
        context = jnp.einsum(
            "hqk,khd->qhd", soft_rows, value_rows, preferred_element_type=jnp.float32
        )
        return (context.astype(jnp.bfloat16), (row_peak + jnp.log(exp_total))[..., 0])

    starts = jnp.arange(length // block_rows, dtype=jnp.int32) * block_rows
    context, log_total = lax.map(one_block, starts)
    return (context.reshape(length, queries.shape[1] * queries.shape[2]), log_total)


def attend_backward(queries, key_rows, value_rows, grad_context, log_total, prefix, block_rows):
    length = key_rows.shape[0]
    score_scale = HEAD_DIM ** (-0.5)

    def one_block(carried, inputs):
        grad_keys, grad_values = carried
        start_row, block_log = inputs
        query_blk, scores = block_scores(queries, key_rows, start_row, block_rows, prefix)
        soft_rows = jnp.exp(scores - block_log[..., None])
        grad_blk = lax.dynamic_slice_in_dim(grad_context, start_row, block_rows, 0)
        grad_soft = jnp.einsum(
            "qhd,khd->hqk", grad_blk, value_rows, preferred_element_type=jnp.float32
        )
        inner_sum = jnp.sum(soft_rows * grad_soft, axis=-1, keepdims=True)
        grad_scores = (soft_rows * (grad_soft - inner_sum)).astype(jnp.bfloat16)
        grad_values = grad_values + jnp.einsum(
            "hqk,qhd->khd",
            soft_rows.astype(jnp.bfloat16),
            grad_blk,
            preferred_element_type=jnp.float32,
        )
        grad_keys = grad_keys + score_scale * jnp.einsum(
            "hqk,qhd->khd", grad_scores, query_blk, preferred_element_type=jnp.float32
        )
        grad_query = score_scale * jnp.einsum(
            "hqk,khd->qhd", grad_scores, key_rows, preferred_element_type=jnp.float32
        )
        return ((grad_keys, grad_values), grad_query)

    empty_rows = jnp.zeros(key_rows.shape, jnp.float32)
    starts = jnp.arange(length // block_rows, dtype=jnp.int32) * block_rows
    (grad_keys, grad_values), grad_query = lax.scan(
        one_block, (empty_rows, empty_rows), (starts, log_total)
    )
    return (
        grad_query.reshape(length, -1),
        grad_keys.reshape(length, -1),
        grad_values.reshape(length, -1),
    )


def to_homes(part_out, expert_size):
    local_experts, row_total, width = part_out.shape
    moved = part_out.reshape(local_experts, expert_size, -1, width).transpose(1, 0, 2, 3)
    return moved.reshape(expert_size * local_experts, -1, width)


def body(
    tokens,
    first_gain,
    second_gain,
    query_weight,
    key_weight,
    value_weight,
    output_weight,
    router_weight,
    expert_in,
    expert_out,
    cotangent,
    routes,
    priority,
    prefix_len,
):
    row_count, width = tokens.shape
    tensor_size = lax.axis_size("tensor")
    expert_size = lax.axis_size("expert")
    length = row_count * tensor_size
    block_rows = min(512, length)
    head_count = query_weight.shape[1] // HEAD_DIM
    experts = router_weight.shape[1]
    groups = row_count // GROUP
    capacity = (5 * GROUP * TOP + 4 * experts - 1) // (4 * experts)
    prefix = prefix_len[0]
    stream = tokens.astype(jnp.float32)
    scaled_one, spread_one, normed_one = norm_rows(stream, first_gain)
    sequence = lax.all_gather(normed_one.astype(jnp.bfloat16), "tensor", axis=0, tiled=True)
    queries = jnp.dot(sequence, query_weight, preferred_element_type=jnp.float32).astype(
        jnp.bfloat16
    )
    key_rows = jnp.dot(sequence, key_weight, preferred_element_type=jnp.float32).astype(
        jnp.bfloat16
    )
    value_rows = jnp.dot(sequence, value_weight, preferred_element_type=jnp.float32).astype(
        jnp.bfloat16
    )
    query_heads = queries.reshape(length, head_count, HEAD_DIM)
    key_heads = key_rows.reshape(length, head_count, HEAD_DIM)
    value_heads = value_rows.reshape(length, head_count, HEAD_DIM)
    context, log_total = attend_forward(query_heads, key_heads, value_heads, prefix, block_rows)
    attended = lax.psum_scatter(
        jnp.dot(context, output_weight, preferred_element_type=jnp.float32).astype(jnp.bfloat16),
        "tensor",
        scatter_dimension=0,
        tiled=True,
    ).astype(jnp.float32)
    residual = stream + attended
    scaled_two, spread_two, normed_two = norm_rows(residual, second_gain)
    mixer_in = normed_two.astype(jnp.bfloat16)
    logits = jnp.dot(mixer_in, router_weight, preferred_element_type=jnp.float32)
    member = jnp.sum(
        (routes[:, :, None] == jnp.arange(experts, dtype=jnp.int32)).astype(jnp.float32), axis=1
    )
    member = member.reshape(groups, GROUP, experts)
    earlier = (priority[:, :, None] < priority[:, None, :]).astype(jnp.float32)
    order_rank = jnp.einsum("gst,gse->gte", earlier, member)
    kept_pairs = member * (order_rank < capacity).astype(jnp.float32)
    exp_terms = kept_pairs * jnp.exp(logits.reshape(groups, GROUP, experts))
    exp_total = jnp.sum(exp_terms, axis=1, keepdims=True)
    kept_count = jnp.sum(kept_pairs, axis=1, keepdims=True)
    weights = exp_terms / jnp.where(kept_count > 0, exp_total, 1.0)
    weights_low = weights.astype(jnp.bfloat16)
    grouped = mixer_in.reshape(groups, GROUP, width)
    mixed_rows = jnp.einsum(
        "gte,gtd->egd", weights_low, grouped, preferred_element_type=jnp.float32
    ).astype(jnp.bfloat16)
    sequence_mix = lax.all_gather(mixed_rows, "tensor", axis=1, tiled=True)
    owner_rows = lax.all_to_all(sequence_mix, "expert", split_axis=0, concat_axis=1, tiled=True)
    hidden_pre = jnp.einsum(
        "erd,edf->erf", owner_rows, expert_in, preferred_element_type=jnp.float32
    )
    sigma_pre = jax.nn.sigmoid(hidden_pre)
    hidden = (hidden_pre * sigma_pre).astype(jnp.bfloat16)
    part_out = jnp.einsum("erf,efd->erd", hidden, expert_out, preferred_element_type=jnp.float32)
    arrived = lax.all_to_all(
        to_homes(part_out, expert_size).astype(jnp.bfloat16),
        "expert",
        split_axis=0,
        concat_axis=0,
        tiled=True,
    )
    summed = lax.psum_scatter(arrived, "tensor", scatter_dimension=1, tiled=True).astype(
        jnp.float32
    )
    returned = summed.astype(jnp.bfloat16)
    mixed_back = jnp.einsum(
        "gte,egd->gtd", weights_low, returned, preferred_element_type=jnp.float32
    ).reshape(row_count, width)
    layer_output = (residual + mixed_back).astype(jnp.bfloat16)
    grad_mix = cotangent.astype(jnp.bfloat16).reshape(groups, GROUP, width)
    grad_returned = jnp.einsum(
        "gte,gtd->egd", weights_low, grad_mix, preferred_element_type=jnp.float32
    ).astype(jnp.bfloat16)
    grad_weights = jnp.einsum(
        "gtd,egd->gte", grad_mix, returned, preferred_element_type=jnp.float32
    )
    sequence_grad = lax.all_gather(grad_returned, "tensor", axis=1, tiled=True)
    grad_owner = lax.all_to_all(sequence_grad, "expert", split_axis=0, concat_axis=1, tiled=True)
    grad_hidden = jnp.einsum(
        "erd,efd->erf", grad_owner, expert_out, preferred_element_type=jnp.float32
    )
    slope = sigma_pre * (1.0 + hidden_pre * (1.0 - sigma_pre))
    grad_pre = (grad_hidden * slope).astype(jnp.bfloat16)
    expert_out_grad = jnp.einsum(
        "erf,erd->efd", hidden, grad_owner, preferred_element_type=jnp.float32
    )
    expert_in_grad = jnp.einsum(
        "erd,erf->edf", owner_rows, grad_pre, preferred_element_type=jnp.float32
    )
    grad_part = jnp.einsum("erf,edf->erd", grad_pre, expert_in, preferred_element_type=jnp.float32)
    grad_arrived = lax.all_to_all(
        to_homes(grad_part, expert_size).astype(jnp.bfloat16),
        "expert",
        split_axis=0,
        concat_axis=0,
        tiled=True,
    )
    grad_summed = lax.psum_scatter(grad_arrived, "tensor", scatter_dimension=1, tiled=True).astype(
        jnp.float32
    )
    grad_mixed = grad_summed.astype(jnp.bfloat16)
    grad_grouped = jnp.einsum(
        "gte,egd->gtd", weights_low, grad_mixed, preferred_element_type=jnp.float32
    )
    grad_weights = grad_weights + jnp.einsum(
        "egd,gtd->gte", grad_mixed, grouped, preferred_element_type=jnp.float32
    )
    inner_sum = jnp.sum(weights * grad_weights, axis=1, keepdims=True)
    grad_logits = (
        (weights * (grad_weights - inner_sum)).reshape(row_count, experts).astype(jnp.bfloat16)
    )
    router_part = jnp.einsum("td,te->de", mixer_in, grad_logits, preferred_element_type=jnp.float32)
    grad_mixer = grad_grouped.reshape(row_count, width) + jnp.einsum(
        "te,de->td", grad_logits, router_weight, preferred_element_type=jnp.float32
    )
    second_part = jnp.sum(grad_mixer * scaled_two, axis=0)
    grad_residual = cotangent + norm_back(grad_mixer, scaled_two, spread_two, second_gain)
    grad_sequence = lax.all_gather(grad_residual.astype(jnp.bfloat16), "tensor", axis=0, tiled=True)
    output_part = jnp.einsum(
        "lc,ld->cd", context, grad_sequence, preferred_element_type=jnp.float32
    )
    grad_context = jnp.einsum(
        "ld,cd->lc", grad_sequence, output_weight, preferred_element_type=jnp.float32
    ).astype(jnp.bfloat16)
    grad_query, grad_keys, grad_values = attend_backward(
        query_heads,
        key_heads,
        value_heads,
        grad_context.reshape(length, head_count, HEAD_DIM),
        log_total,
        prefix,
        block_rows,
    )
    grad_query = grad_query.astype(jnp.bfloat16)
    grad_keys = grad_keys.astype(jnp.bfloat16)
    grad_values = grad_values.astype(jnp.bfloat16)
    query_part = jnp.einsum("ld,lc->dc", sequence, grad_query, preferred_element_type=jnp.float32)
    key_part = jnp.einsum("ld,lc->dc", sequence, grad_keys, preferred_element_type=jnp.float32)
    value_part = jnp.einsum("ld,lc->dc", sequence, grad_values, preferred_element_type=jnp.float32)
    total_grad = jnp.einsum(
        "lc,dc->ld", grad_query, query_weight, preferred_element_type=jnp.float32
    )
    total_grad = total_grad + jnp.einsum(
        "lc,dc->ld", grad_keys, key_weight, preferred_element_type=jnp.float32
    )
    grad_normed = lax.psum_scatter(
        (
            total_grad
            + jnp.einsum("lc,dc->ld", grad_values, value_weight, preferred_element_type=jnp.float32)
        ).astype(jnp.bfloat16),
        "tensor",
        scatter_dimension=0,
        tiled=True,
    ).astype(jnp.float32)
    first_part = jnp.sum(grad_normed * scaled_one, axis=0)
    tokens_grad = grad_residual + norm_back(grad_normed, scaled_one, spread_one, first_gain)
    query_grad, key_grad, value_grad, output_grad = (
        lax.psum(query_part.astype(jnp.bfloat16), "expert").astype(jnp.float32),
        lax.psum(key_part.astype(jnp.bfloat16), "expert").astype(jnp.float32),
        lax.psum(value_part.astype(jnp.bfloat16), "expert").astype(jnp.float32),
        lax.psum(output_part.astype(jnp.bfloat16), "expert").astype(jnp.float32),
    )
    first_gain_grad, second_gain_grad, router_grad = lax.psum(
        (first_part, second_part, router_part), ("expert", "tensor")
    )
    return (
        layer_output,
        tokens_grad,
        first_gain_grad,
        second_gain_grad,
        query_grad,
        key_grad,
        value_grad,
        output_grad,
        router_grad,
        expert_in_grad,
        expert_out_grad,
    )


def solution(mesh):
    in_specs = (
        P(("expert", "tensor"), None),
        P(),
        P(),
        P(None, "tensor"),
        P(None, "tensor"),
        P(None, "tensor"),
        P("tensor", None),
        P(),
        P("expert", None, "tensor"),
        P("expert", "tensor", None),
        P(("expert", "tensor"), None),
        P(("expert", "tensor"), None),
        P(("expert", "tensor"), None),
        P("expert"),
    )
    out_specs = (
        P(("expert", "tensor"), None),
        P(("expert", "tensor"), None),
        P(),
        P(),
        P(None, "tensor"),
        P(None, "tensor"),
        P(None, "tensor"),
        P("tensor", None),
        P(),
        P("expert", None, "tensor"),
        P("expert", "tensor", None),
    )
    return jax.shard_map(body, mesh=mesh, in_specs=in_specs, out_specs=out_specs, check_vma=False)
```

profile of v0, /device:TPU:1, one launch (start us, length us, event | category | flops | bytes accessed | tf_op | source)
XLA Modules:
  0.0 777.5 jit_solution(236218361544068434)
XLA Ops:
  12.6 33.8 %all-gather.5.cloned.1.call-done = bf16[2048,512]{1,0:T(8,128)(2,1)} async-done(((bf16[512,512]{1,0:T(8,128)(2,1)}), bf16[2048,512]{1,0:T(8,128)(2,1)}) %all-gather.5.cloned.1.call-update) | async-done | bytes 2097168 | tf_op jit(solution)/shard_map/all_gather | solution.py:131
  53.1 56.4 %while.27 = (s32[]{:T(128)}, bf16[4,512,2,64]{1,3,2,0:T(8,128)(2,1)S(1)}, f32[4,2,512]{2,1,0:T(2,128)}, s32[4]{0:T(128)}, s32[]{:T(128)}, /*index=5*/bf16[2048,2...) while((s32[]{:T(128)}, ...), condition=%wide.region_5.6_spmd, body=%wide.region_2.5_spmd.sunk | while | flops 564200960 | bytes 30711992 | solution.py:52
  58.4 3.1 fusion.162
  72.5 3.1 fusion.162
  86.6 3.0 fusion.162
  113.2 29.8 %reduce-scatter.5.cloned.1.call-done = bf16[512,512]{1,0:T(8,128)(2,1)} async-done(((bf16[2048,512]{1,0:T(8,128)(2,1)}), bf16[512,512]{1,0:T(8,128)(2,1)}) %reduce-scatter.5.cloned.1.call-update) | async-done | bytes 524304 | tf_op jit(solution)/shard_map/reduce_scatter | solution.py:145
  151.3 28.2 %all-gather.7.cloned.1.call-done = bf16[32,64,512]{2,0,1:T(8,128)(2,1)} async-done(((bf16[32,16,512]{2,0,1:T(8,128)(2,1)}), bf16[32,64,512]{2,0,1:T(8,128)(2,1)}) %all-gather.7.cloned.1.call-update) | async-done | bytes 2097168 | tf_op jit(solution)/shard_map/all_gather | solution.py:171
  179.5 4.1 copy.64
  183.6 8.1 %all-to-all-start = ((bf16[32,64,512]{2,1,0:T(8,128)(2,1)}), bf16[32,64,512]{2,1,0:T(8,128)(2,1)}, u32[]{:S(2)}, u32[]{:S(2)}) async-start(bf16[32,64,512]{2,1,0:T(8,128)(2,1)} %copy.64), calls=%async_computation.1 | async-start | bytes 4194304 | tf_op jit(solution)/shard_map/all_to_all | solution.py:172
  191.7 21.0 %all-gather.9.cloned.1.call-done = bf16[32,64,512]{2,0,1:T(8,128)(2,1)} async-done(((bf16[32,16,512]{2,0,1:T(8,128)(2,1)}), bf16[32,64,512]{2,0,1:T(8,128)(2,1)}) %all-gather.9.cloned.1.call-update) | async-done | bytes 2097168 | tf_op jit(solution)/shard_map/all_gather | solution.py:201
  212.7 4.1 copy.67
  216.8 3.2 all-to-all-done
  220.0 5.2 all-to-all-start.2
  225.3 6.0 multiply_convert_fusion.2
  231.3 22.4 %all-to-all-done.2 = bf16[32,64,512]{2,1,0:T(8,128)(2,1)} async-done(((bf16[32,64,512]{2,1,0:T(8,128)(2,1)}), bf16[32,64,512]{2,1,0:T(8,128)(2,1)}, u32[]{:S(2)}, u32[]{:S(2)}) %all-to-all-start.2) | async-done | bytes 2097184 | tf_op jit(solution)/shard_map/all_to_all | solution.py:202
  253.7 5.2 multiply_convert_fusion.1
  261.6 32.6 %all_to_all.28 = bf16[32,64,512]{2,1,0:T(8,128)(2,1)} all-to-all(bf16[32,64,512]{2,1,0:T(8,128)(2,1)S(1)} %convolution_convert_fusion.5), channel_id=1, replica_groups=mesh['expert'=32,'tensor'=4] {'expert'}, dimensions={0} | all-to-all | bytes 4194304 | tf_op jit(solution)/shard_map/all_to_all | solution.py:215
  297.1 32.0 %all_to_all.29 = bf16[32,64,512]{2,1,0:T(8,128)(2,1)} all-to-all(bf16[32,64,512]{2,1,0:T(8,128)(2,1)S(1)} %convolution_convert_fusion.6), channel_id=1, replica_groups=mesh['expert'=32,'tensor'=4] {'expert'}, dimensions={0} | all-to-all | bytes 4194304 | tf_op jit(solution)/shard_map/all_to_all | solution.py:179
  331.5 24.1 %reduce-scatter.7.cloned.1.call-done = bf16[32,16,512]{2,1,0:T(8,128)(2,1)} async-done(((bf16[32,64,512]{2,1,0:T(8,128)(2,1)}), bf16[32,16,512]{2,1,0:T(8,128)(2,1)}) %reduce-scatter.7.cloned.1.call-update) | async-done | bytes 524304 | tf_op jit(solution)/shard_map/reduce_scatter | solution.py:186
  362.9 30.5 %all-gather.11.cloned.1.call-done = bf16[2048,512]{1,0:T(8,128)(2,1)} async-done(((bf16[512,512]{1,0:T(8,128)(2,1)}), bf16[2048,512]{1,0:T(8,128)(2,1)}) %all-gather.11.cloned.1.call-update) | async-done | bytes 2097168 | tf_op jit(solution)/shard_map/all_gather | solution.py:242
  395.8 81.7 %while.28 = (s32[]{:T(128)}, f32[2048,2,64]{0,2,1:T(8,128)S(1)}, f32[2048,2,64]{0,2,1:T(8,128)}, bf16[4,512,2,64]{1,3,2,0:T(8,128)(2,1)}, s32[4]{0:T(128)}, /*in...) while((s32[]{:T(128)}, f32[2048,2,64]{0,2,1:T(8,128)S(1)}, ...), condition=%wide.region_19.20_spmd.clone, body=%wide.region_17.19_spmd.clone.sunk | while | flops 1377109504 | bytes 86282592 | solution.py:87
  406.8 3.2 multiply_reduce_fusion.7
  427.2 3.2 multiply_reduce_fusion.7
  447.6 3.2 multiply_reduce_fusion.7
  468.0 3.2 multiply_reduce_fusion.7
  490.3 5.5 add_convert_fusion
  495.9 4.6 convolution_bitcast_fusion
  500.6 4.0 convolution_bitcast_fusion.1
  505.5 88.3 %all-reduce.7.cloned.1.call-done = (bf16[512,128]{1,0:T(8,128)(2,1)}, bf16[512,128]{1,0:T(8,128)(2,1)}, bf16[512,128]{1,0:T(8,128)(2,1)}, bf16[128,512]{1,0:T(8,128)(2,1)}) async-done(((bf16[512,128]{1,0:T(8,128)(2,1)}, bf16[512,128]{1,0:T(8,128)(2,1)}, bf16[512,128]{1,0:T(8,128)(2,1)}, bf16[128,512]{1,0:T(8,128)(2,1)}), (bf16[512,128]{1,0:T(8,128)(2,1)}, bf16[512,128]{1,0:T(8,128)(2,1)}, ...) | async-done | bytes 524304 | tf_op jit(solution)/shard_map/psum | solution.py:282
  600.3 25.5 %reduce-scatter.11.cloned.1.call-done = bf16[512,512]{1,0:T(8,128)(2,1)} async-done(((bf16[2048,512]{1,0:T(8,128)(2,1)}), bf16[512,512]{1,0:T(8,128)(2,1)}) %reduce-scatter.11.cloned.1.call-update) | async-done | bytes 524304 | tf_op jit(solution)/shard_map/reduce_scatter | solution.py:270
  629.9 64.7 %all-reduce = (f32[512]{0:T(512)}, f32[512]{0:T(512)}) all-reduce(f32[512]{0:T(512)S(1)} %get-tuple-element.156, f32[512]{0:T(512)S(1)} %get-tuple-element.154), channel_id=1, replica_groups=mesh['expert'=32,'tensor'=4] {'expert','tensor'}, use_global_device_ids=true, to_apply=%region_24.25 | all-reduce | flops 1024 | bytes 8192 | tf_op jit(solution)/shard_map/psum | solution.py:287
  694.5 74.4 %all-reduce.5.cloned.1.call-done = f32[512,32]{0,1:T(8,128)} async-done(((f32[512,32]{0,1:T(8,128)}), f32[512,32]{0,1:T(8,128)}) %all-reduce.5.cloned.1.call-update) | async-done | bytes 65552 | tf_op jit(solution)/shard_map/psum | solution.py:287
  (261 shorter events, 166.7 us)
Async XLA Ops:
  7.2 218.1 %copy-start = (bf16[1,512,512]{2,1,0:T(8,128)(2,1)S(1)}, bf16[1,512,512]{2,1,0:T(8,128)(2,1)}, u32[]{:S(2)}) copy-start(bf16[1,512,512]{2,1,0:T(8,128)(2,1)} %param.26) | copy-start | bytes 1572868
  7.2 41.8 %copy-start.22 = (bf16[512,128]{1,0:T(8,128)(2,1)S(1)}, bf16[512,128]{1,0:T(8,128)(2,1)}, u32[]{:S(2)}) copy-start(bf16[512,128]{1,0:T(8,128)(2,1)} %param.22) | copy-start | bytes 393220
  7.2 44.2 %copy-start.24 = (bf16[512,128]{1,0:T(8,128)(2,1)S(1)}, bf16[512,128]{1,0:T(8,128)(2,1)}, u32[]{:S(2)}) copy-start(bf16[512,128]{1,0:T(8,128)(2,1)} %param.21) | copy-start | bytes 393220
  7.2 39.2 %all-gather.5.cloned.1.call-start = ((), (), s32[]{:S(2)}) async-start(), calls=%async_computation.8 | async-start | bytes 2621440 | tf_op jit(solution)/shard_map/all_gather | solution.py:131
  8.5 44.5 %copy-start.30 = (f32[512]{0:T(512)}, f32[512]{0:T(512)S(1)}, u32[]{:S(2)}) copy-start(f32[512]{0:T(512)S(1)} %broadcast_multiply_fusion.5) | copy-start | bytes 6148
  9.9 43.2 %copy-start.33 = (f32[512]{0:T(512)}, f32[512]{0:T(512)S(1)}, u32[]{:S(2)}) copy-start(f32[512]{0:T(512)S(1)} %add_rsqrt_fusion.1) | copy-start | bytes 6148
  12.0 130.9 %reduce-scatter.5.cloned.1.call-start = ((), (), s32[]{:S(2)}) async-start(), calls=%async_computation.9 | async-start | bytes 2621440 | tf_op jit(solution)/shard_map/reduce_scatter | solution.py:145
  53.1 57.8 %copy-start.26 = (bf16[128,512]{1,0:T(8,128)(2,1)S(1)}, bf16[128,512]{1,0:T(8,128)(2,1)}, u32[]{:S(2)}) copy-start(bf16[128,512]{1,0:T(8,128)(2,1)} %param.24) | copy-start | bytes 393220
  109.5 33.4 %copy-start.4 = (bf16[512,512]{1,0:T(8,128)(2,1)S(1)}, bf16[512,512]{1,0:T(8,128)(2,1)}, u32[]{:S(2)}) copy-start(bf16[512,512]{1,0:T(8,128)(2,1)} %param.18) | copy-start | bytes 1572868
  109.9 35.6 %copy-start.35 = (f32[512]{0:T(512)S(1)}, f32[512]{0:T(512)}, u32[]{:S(2)}) copy-start(f32[512]{0:T(512)} %param.20) | copy-start | bytes 6148
  110.9 36.0 %copy-start.28 = (bf16[512,32]{0,1:T(8,128)(2,1)S(1)}, bf16[512,32]{0,1:T(8,128)(2,1)}, u32[]{:S(2)}) copy-start(bf16[512,32]{0,1:T(8,128)(2,1)} %param.25) | copy-start | bytes 98308
  112.9 34.3 %copy-start.32 = (s32[16,32]{1,0:T(8,128)S(1)}, s32[16,32]{1,0:T(8,128)}, u32[]{:S(2)}) copy-start(s32[16,32]{1,0:T(8,128)} %param.30) | copy-start | bytes 6148
  113.0 66.5 %all-gather.7.cloned.1.call-start = ((), (), s32[]{:S(2)}) async-start(), calls=%async_computation.10 | async-start | bytes 2621440 | tf_op jit(solution)/shard_map/all_gather | solution.py:171
  146.9 182.4 %copy-start.5 = (bf16[512,512]{1,0:T(8,128)(2,1)}, bf16[512,512]{1,0:T(8,128)(2,1)S(1)}, u32[]{:S(2)}) copy-start(bf16[512,512]{1,0:T(8,128)(2,1)S(1)} %multiply_convert_fusion.3) | copy-start | bytes 1572868
  148.8 63.9 %all-gather.9.cloned.1.call-start = ((), (), s32[]{:S(2)}) async-start(), calls=%async_computation.12 | async-start | bytes 2621440 | tf_op jit(solution)/shard_map/all_gather | solution.py:201
  183.6 36.4 %all-to-all-start = ((bf16[32,64,512]{2,1,0:T(8,128)(2,1)}), bf16[32,64,512]{2,1,0:T(8,128)(2,1)}, u32[]{:S(2)}, u32[]{:S(2)}) async-start(bf16[32,64,512]{2,1,0:T(8,128)(2,1)} %copy.64), calls=%async_computation.1 | async-start | bytes 4194304 | tf_op jit(solution)/shard_map/all_to_all | solution.py:172
  220.0 33.7 %all-to-all-start.2 = ((bf16[32,64,512]{2,1,0:T(8,128)(2,1)}), bf16[32,64,512]{2,1,0:T(8,128)(2,1)}, u32[]{:S(2)}, u32[]{:S(2)}) async-start(bf16[32,64,512]{2,1,0:T(8,128)(2,1)} %copy.67), calls=%async_computation.4 | async-start | bytes 4194304 | tf_op jit(solution)/shard_map/all_to_all | solution.py:202
  225.2 104.0 %reduce-scatter.9.cloned.1.call-start = ((), (), s32[]{:S(2)}) async-start(), calls=%async_computation.13 | async-start | bytes 2621440 | tf_op jit(solution)/shard_map/reduce_scatter | solution.py:222
  261.6 32.7 %copy-start.39 = (bf16[1,512,512]{2,1,0:T(8,128)(2,1)S(1)}, bf16[1,512,512]{2,1,0:T(8,128)(2,1)}, u32[]{:S(2)}) copy-start(bf16[1,512,512]{2,1,0:T(8,128)(2,1)} %param.27) | copy-start | bytes 1572868
  294.2 61.3 %reduce-scatter.7.cloned.1.call-start = ((), (), s32[]{:S(2)}) async-start(), calls=%async_computation.11 | async-start | bytes 2621440 | tf_op jit(solution)/shard_map/reduce_scatter | solution.py:186
  329.1 29.8 %copy-start.7 = (bf16[512,512]{1,0:T(8,128)(2,1)S(1)}, bf16[512,512]{1,0:T(8,128)(2,1)}, u32[]{:S(2)}) copy-start(bf16[512,512]{1,0:T(8,128)(2,1)} %reduce-scatter.5.cloned.1.call-done) | copy-start | bytes 1572868
  329.1 64.3 %all-gather.11.cloned.1.call-start = ((), (), s32[]{:S(2)}) async-start(), calls=%async_computation.14 | async-start | bytes 2621440 | tf_op jit(solution)/shard_map/all_gather | solution.py:242
  331.5 27.5 %copy-start.29 = (bf16[512,32]{0,1:T(8,128)(2,1)S(1)}, bf16[512,32]{0,1:T(8,128)(2,1)}, u32[]{:S(2)}) copy-start(bf16[512,32]{0,1:T(8,128)(2,1)} %param.25) | copy-start | bytes 98308
  360.3 33.1 %copy-start.27 = (bf16[128,512]{1,0:T(8,128)(2,1)S(1)}, bf16[128,512]{1,0:T(8,128)(2,1)}, u32[]{:S(2)}) copy-start(bf16[128,512]{1,0:T(8,128)(2,1)} %param.24) | copy-start | bytes 393220
  362.7 231.1 %all-reduce.7.cloned.1.call-start = ((), (), s32[]{:S(2)}) async-start(), calls=%async_computation.17 | async-start | bytes 1048576 | tf_op jit(solution)/shard_map/psum | solution.py:282
  490.2 135.5 %reduce-scatter.11.cloned.1.call-start = ((), (), s32[]{:S(2)}) async-start(), calls=%async_computation.15 | async-start | bytes 2621440 | tf_op jit(solution)/shard_map/reduce_scatter | solution.py:270
  495.8 273.1 %all-reduce.5.cloned.1.call-start = ((), (), s32[]{:S(2)}) async-start(), calls=%async_computation.16 | async-start | bytes 131072 | tf_op jit(solution)/shard_map/psum | solution.py:287
  500.5 125.2 %copy-start.31 = (f32[512]{0:T(512)S(1)}, f32[512]{0:T(512)}, u32[]{:S(2)}) copy-start(f32[512]{0:T(512)} %copy-done.30) | copy-start | bytes 6148
  500.5 125.2 %copy-start.34 = (f32[512]{0:T(512)S(1)}, f32[512]{0:T(512)}, u32[]{:S(2)}) copy-start(f32[512]{0:T(512)} %copy-done.33) | copy-start | bytes 6148
  500.5 125.2 %copy-start.37 = (f32[512]{0:T(512)S(1)}, f32[512]{0:T(512)}, u32[]{:S(2)}) copy-start(f32[512]{0:T(512)} %param.19) | copy-start | bytes 6148
  500.5 126.9 %copy-start.12 = (f32[512,512]{1,0:T(8,128)S(1)}, f32[512,512]{1,0:T(8,128)}, u32[]{:S(2)}) copy-start(f32[512,512]{1,0:T(8,128)} %get-tuple-element.205) | copy-start | bytes 3145732
  500.6 269.9 %copy-start.1 = (bf16[1,512,512]{2,1,0:T(8,128)(2,1)S(1)}, bf16[1,512,512]{2,1,0:T(8,128)(2,1)}, u32[]{:S(2)}) copy-start(bf16[1,512,512]{2,1,0:T(8,128)(2,1)} %param.26) | copy-start | bytes 1572868
  (34 other events, 105.9 us)
Sparse Core Ops, SparseCore 0:
  12.1 34.2 all-gather.4
  113.1 29.8 reduce-scatter.4
  148.9 30.5 all-gather.6
  181.7 30.9 all-gather.8
  294.3 26.2 reduce-scatter.8
  329.3 26.2 reduce-scatter.6
  362.8 30.5 all-gather.10
  490.3 103.3 all-reduce.6
  596.2 29.5 reduce-scatter.10
  631.6 137.2 all-reduce.4
where the time goes:
time: 788 us; the launch traced here: 778 us
  waiting for transfers between devices  381 us (48%)
  matrix products  132 us (17%)
  blocking collectives  129 us (16%)
  other arithmetic  62.2 us (8%)
  local copies, waits for them, and re-layouts  27.2 us (3%)
  loops' own time  16.4 us (2%)
  between operations  15.1 us (2%)
  starting transfers between devices  13.9 us (2%)
    psum x1, waiting for transfers between devices, body(): lax.psum(query_part.astype(jnp.bfloat16), 'expert').astype(jnp.float32)  88.3 us
    psum x1, waiting for transfers between devices, body(): lax.psum((first_part, second_part, router_part), ('expert', 'tensor'))  74.4 us
    psum x1, blocking collectives, body(): lax.psum((first_part, second_part, router_part), ('expert', 'tensor'))  64.7 us
    all_gather x1, waiting for transfers between devices, body(): lax.all_gather(normed_one.astype(jnp.bfloat16), 'tensor', axis=0, tiled=T...  33.8 us
    all_to_all x1, blocking collectives, body(): lax.all_to_all(to_homes(grad_part, expert_size).astype(jnp.bfloat16), 'ex...  32.6 us
    all_to_all x1, blocking collectives, body(): lax.all_to_all(to_homes(part_out, expert_size).astype(jnp.bfloat16), 'exp...  32 us
    all_gather x1, waiting for transfers between devices, body(): lax.all_gather(grad_residual.astype(jnp.bfloat16), 'tensor', axis=0, tile...  30.5 us
    reduce_scatter x1, waiting for transfers between devices, body(): lax.psum_scatter(jnp.dot(context, output_weight, preferred_element_type=j...  29.8 us
  transfers between devices with their start and end apart: 12, of which 11 were waited for; matrix products, arithmetic and copies ran while one was open for 6% of the time, Pallas kernels for 0%

commit v1 on v0

--- a/solution.py
+++ b/solution.py
@@ -285,7 +285,7 @@
         lax.psum(output_part.astype(jnp.bfloat16), "expert").astype(jnp.float32),
     )
     first_gain_grad, second_gain_grad, router_grad = lax.psum(
-        (first_part, second_part, router_part), ("expert", "tensor")
+        lax.psum((first_part, second_part, router_part), "tensor"), "expert"
     )
     return (
         layer_output,

time: 788 us -> 743 us (0.943)
  waiting for transfers between devices: 381 us -> 329 us
    psum x1 -> x2, waiting for transfers between devices: 74.4 us -> 22.7 us  [the longest x1 22.7 us: body(): lax.psum(lax.psum((first_part, second_part, router_part), 'tensor'), 'exp...]
    psum x1 -> x2, blocking collectives: 64.7 us -> 71.7 us  [the longest x1 65.2 us: body(): lax.psum(lax.psum((first_part, second_part, router_part), 'tensor'), 'exp...]
  transfers between devices with their start and end apart: 12 -> 13, of which waited for: 11 -> 11; matrix products, arithmetic and copies ran while one was open for 6% -> 19% of each run, Pallas kernels for 0% -> 0%
where the time goes in v1:
time: 743 us; the launch traced here: 732 us
  waiting for transfers between devices  329 us (44%)
  blocking collectives  136 us (18%)
  matrix products  132 us (18%)
  other arithmetic  62.2 us (8%)
  local copies, waits for them, and re-layouts  28 us (4%)
  loops' own time  16.4 us (2%)
  between operations  14.8 us (2%)
  starting transfers between devices  13.9 us (2%)
    psum x1, waiting for transfers between devices, body(): lax.psum(query_part.astype(jnp.bfloat16), 'expert').astype(jnp.float32)  89.3 us
    psum x1, blocking collectives, body(): lax.psum(lax.psum((first_part, second_part, router_part), 'tensor'), 'exp...  65.2 us
    all_gather x1, waiting for transfers between devices, body(): lax.all_gather(normed_one.astype(jnp.bfloat16), 'tensor', axis=0, tiled=T...  33.8 us
    all_to_all x1, blocking collectives, body(): lax.all_to_all(to_homes(grad_part, expert_size).astype(jnp.bfloat16), 'ex...  32.5 us
    all_to_all x1, blocking collectives, body(): lax.all_to_all(to_homes(part_out, expert_size).astype(jnp.bfloat16), 'exp...  32.1 us
    reduce_scatter x1, waiting for transfers between devices, body(): lax.psum_scatter(jnp.dot(context, output_weight, preferred_element_type=j...  29.8 us
    all_gather x1, waiting for transfers between devices, body(): lax.all_gather(grad_residual.astype(jnp.bfloat16), 'tensor', axis=0, tile...  29.5 us
    all_gather x1, waiting for transfers between devices, body(): sequence_mix = lax.all_gather(mixed_rows, 'tensor', axis=1, tiled=True)  27.4 us
  transfers between devices with their start and end apart: 13, of which 11 were waited for; matrix products, arithmetic and copies ran while one was open for 19% of the time, Pallas kernels for 0%

profile of v1, /device:TPU:1, one launch (start us, length us, event | category | flops | bytes accessed | tf_op | source)
XLA Modules:
  0.0 732.3 jit_solution(5763961517404616485)
XLA Ops:
  12.6 33.8 %all-gather.5.cloned.1.call-done = bf16[2048,512]{1,0:T(8,128)(2,1)} async-done(((bf16[512,512]{1,0:T(8,128)(2,1)}), bf16[2048,512]{1,0:T(8,128)(2,1)}) %all-gather.5.cloned.1.call-update) | async-done | bytes 2097168 | tf_op jit(solution)/shard_map/all_gather | solution.py:131
  53.1 56.4 %while.27 = (s32[]{:T(128)}, bf16[4,512,2,64]{1,3,2,0:T(8,128)(2,1)S(1)}, f32[4,2,512]{2,1,0:T(2,128)}, s32[4]{0:T(128)}, s32[]{:T(128)}, /*index=5*/bf16[2048,2...) while((s32[]{:T(128)}, ...), condition=%wide.region_5.6_spmd, body=%wide.region_2.5_spmd.sunk | while | flops 564200960 | bytes 30711992 | solution.py:52
  58.4 3.1 fusion.162
  72.5 3.1 fusion.162
  113.2 29.8 %reduce-scatter.5.cloned.1.call-done = bf16[512,512]{1,0:T(8,128)(2,1)} async-done(((bf16[2048,512]{1,0:T(8,128)(2,1)}), bf16[512,512]{1,0:T(8,128)(2,1)}) %reduce-scatter.5.cloned.1.call-update) | async-done | bytes 524304 | tf_op jit(solution)/shard_map/reduce_scatter | solution.py:145
  152.1 27.4 %all-gather.7.cloned.1.call-done = bf16[32,64,512]{2,0,1:T(8,128)(2,1)} async-done(((bf16[32,16,512]{2,0,1:T(8,128)(2,1)}), bf16[32,64,512]{2,0,1:T(8,128)(2,1)}) %all-gather.7.cloned.1.call-update) | async-done | bytes 2097168 | tf_op jit(solution)/shard_map/all_gather | solution.py:171
  179.5 4.1 copy.64
  183.6 8.1 %all-to-all-start = ((bf16[32,64,512]{2,1,0:T(8,128)(2,1)}), bf16[32,64,512]{2,1,0:T(8,128)(2,1)}, u32[]{:S(2)}, u32[]{:S(2)}) async-start(bf16[32,64,512]{2,1,0:T(8,128)(2,1)} %copy.64), calls=%async_computation.1 | async-start | bytes 4194304 | tf_op jit(solution)/shard_map/all_to_all | solution.py:172
  191.6 21.0 %all-gather.9.cloned.1.call-done = bf16[32,64,512]{2,0,1:T(8,128)(2,1)} async-done(((bf16[32,16,512]{2,0,1:T(8,128)(2,1)}), bf16[32,64,512]{2,0,1:T(8,128)(2,1)}) %all-gather.9.cloned.1.call-update) | async-done | bytes 2097168 | tf_op jit(solution)/shard_map/all_gather | solution.py:201
  212.7 4.1 copy.67
  216.8 3.2 all-to-all-done
  220.0 5.2 all-to-all-start.2
  225.3 6.0 multiply_convert_fusion.2
  231.3 22.3 %all-to-all-done.2 = bf16[32,64,512]{2,1,0:T(8,128)(2,1)} async-done(((bf16[32,64,512]{2,1,0:T(8,128)(2,1)}), bf16[32,64,512]{2,1,0:T(8,128)(2,1)}, u32[]{:S(2)}, u32[]{:S(2)}) %all-to-all-start.2) | async-done | bytes 2097184 | tf_op jit(solution)/shard_map/all_to_all | solution.py:202
  253.7 5.1 multiply_convert_fusion.1
  261.4 32.5 %all_to_all.28 = bf16[32,64,512]{2,1,0:T(8,128)(2,1)} all-to-all(bf16[32,64,512]{2,1,0:T(8,128)(2,1)S(1)} %convolution_convert_fusion.5), channel_id=1, replica_groups=mesh['expert'=32,'tensor'=4] {'expert'}, dimensions={0} | all-to-all | bytes 4194304 | tf_op jit(solution)/shard_map/all_to_all | solution.py:215
  296.8 32.1 %all_to_all.29 = bf16[32,64,512]{2,1,0:T(8,128)(2,1)} all-to-all(bf16[32,64,512]{2,1,0:T(8,128)(2,1)S(1)} %convolution_convert_fusion.6), channel_id=1, replica_groups=mesh['expert'=32,'tensor'=4] {'expert'}, dimensions={0} | all-to-all | bytes 4194304 | tf_op jit(solution)/shard_map/all_to_all | solution.py:179
  331.3 24.1 %reduce-scatter.7.cloned.1.call-done = bf16[32,16,512]{2,1,0:T(8,128)(2,1)} async-done(((bf16[32,64,512]{2,1,0:T(8,128)(2,1)}), bf16[32,16,512]{2,1,0:T(8,128)(2,1)}) %reduce-scatter.7.cloned.1.call-update) | async-done | bytes 524304 | tf_op jit(solution)/shard_map/reduce_scatter | solution.py:186
  363.7 29.5 %all-gather.11.cloned.1.call-done = bf16[2048,512]{1,0:T(8,128)(2,1)} async-done(((bf16[512,512]{1,0:T(8,128)(2,1)}), bf16[2048,512]{1,0:T(8,128)(2,1)}) %all-gather.11.cloned.1.call-update) | async-done | bytes 2097168 | tf_op jit(solution)/shard_map/all_gather | solution.py:242
  395.7 81.7 %while.28 = (s32[]{:T(128)}, f32[2048,2,64]{0,2,1:T(8,128)S(1)}, f32[2048,2,64]{0,2,1:T(8,128)}, bf16[4,512,2,64]{1,3,2,0:T(8,128)(2,1)}, s32[4]{0:T(128)}, /*in...) while((s32[]{:T(128)}, f32[2048,2,64]{0,2,1:T(8,128)S(1)}, ...), condition=%wide.region_19.20_spmd.clone, body=%wide.region_17.19_spmd.clone.sunk | while | flops 1377109504 | bytes 86282592 | solution.py:87
  406.7 3.2 multiply_reduce_fusion.7
  427.1 3.2 multiply_reduce_fusion.7
  447.5 3.2 multiply_reduce_fusion.7
  467.8 3.2 multiply_reduce_fusion.7
  490.1 5.5 add_convert_fusion
  495.7 4.6 convolution_bitcast_fusion
  500.4 4.0 convolution_bitcast_fusion.1
  504.4 89.3 %all-reduce.11.cloned.1.call-done = (bf16[512,128]{1,0:T(8,128)(2,1)}, bf16[512,128]{1,0:T(8,128)(2,1)}, bf16[512,128]{1,0:T(8,128)(2,1)}, bf16[128,512]{1,0:T(8,128)(2,1)}) async-done(((bf16[512,128]{1,0:T(8,128)(2,1)}, bf16[512,128]{1,0:T(8,128)(2,1)}, bf16[512,128]{1,0:T(8,128)(2,1)}, bf16[128,512]{1,0:T(8,128)(2,1)}), (bf16[512,128]{1,0:T(8,128)(2,1)}, bf16[512,128]{1,0:T(8,128)(2,1)}, ...) | async-done | bytes 524304 | tf_op jit(solution)/shard_map/psum | solution.py:282
  600.1 25.4 %reduce-scatter.11.cloned.1.call-done = bf16[512,512]{1,0:T(8,128)(2,1)} async-done(((bf16[2048,512]{1,0:T(8,128)(2,1)}), bf16[512,512]{1,0:T(8,128)(2,1)}) %reduce-scatter.11.cloned.1.call-update) | async-done | bytes 524304 | tf_op jit(solution)/shard_map/reduce_scatter | solution.py:270
  629.7 6.5 all-reduce.1
  636.2 65.2 %all-reduce = (f32[512]{0:T(512)}, f32[512]{0:T(512)}) all-reduce(f32[512]{0:T(512)S(1)} %get-tuple-element.200, f32[512]{0:T(512)S(1)} %get-tuple-element.201), channel_id=1, replica_groups=mesh['expert'=32,'tensor'=4] {'expert'}, use_global_device_ids=true, to_apply=%region_25.26 | all-reduce | flops 1024 | bytes 8192 | tf_op jit(solution)/shard_map/psum | solution.py:287
  701.4 22.7 %all-reduce.9.cloned.1.call-done = f32[512,32]{0,1:T(8,128)} async-done(((f32[512,32]{0,1:T(8,128)}), f32[512,32]{0,1:T(8,128)}) %all-reduce.9.cloned.1.call-update) | async-done | bytes 65552 | tf_op jit(solution)/shard_map/psum | solution.py:287
  (269 shorter events, 170.6 us)
Async XLA Ops:
  7.2 218.1 %copy-start = (bf16[1,512,512]{2,1,0:T(8,128)(2,1)S(1)}, bf16[1,512,512]{2,1,0:T(8,128)(2,1)}, u32[]{:S(2)}) copy-start(bf16[1,512,512]{2,1,0:T(8,128)(2,1)} %param.26) | copy-start | bytes 1572868
  7.2 41.8 %copy-start.24 = (bf16[512,128]{1,0:T(8,128)(2,1)S(1)}, bf16[512,128]{1,0:T(8,128)(2,1)}, u32[]{:S(2)}) copy-start(bf16[512,128]{1,0:T(8,128)(2,1)} %param.22) | copy-start | bytes 393220
  7.2 44.2 %copy-start.26 = (bf16[512,128]{1,0:T(8,128)(2,1)S(1)}, bf16[512,128]{1,0:T(8,128)(2,1)}, u32[]{:S(2)}) copy-start(bf16[512,128]{1,0:T(8,128)(2,1)} %param.21) | copy-start | bytes 393220
  7.2 39.2 %all-gather.5.cloned.1.call-start = ((), (), s32[]{:S(2)}) async-start(), calls=%async_computation.8 | async-start | bytes 2621440 | tf_op jit(solution)/shard_map/all_gather | solution.py:131
  8.5 44.5 %copy-start.32 = (f32[512]{0:T(512)}, f32[512]{0:T(512)S(1)}, u32[]{:S(2)}) copy-start(f32[512]{0:T(512)S(1)} %broadcast_multiply_fusion.5) | copy-start | bytes 6148
  9.9 43.2 %copy-start.35 = (f32[512]{0:T(512)}, f32[512]{0:T(512)S(1)}, u32[]{:S(2)}) copy-start(f32[512]{0:T(512)S(1)} %add_rsqrt_fusion.1) | copy-start | bytes 6148
  12.0 130.9 %reduce-scatter.5.cloned.1.call-start = ((), (), s32[]{:S(2)}) async-start(), calls=%async_computation.9 | async-start | bytes 2621440 | tf_op jit(solution)/shard_map/reduce_scatter | solution.py:145
  53.1 57.8 %copy-start.28 = (bf16[128,512]{1,0:T(8,128)(2,1)S(1)}, bf16[128,512]{1,0:T(8,128)(2,1)}, u32[]{:S(2)}) copy-start(bf16[128,512]{1,0:T(8,128)(2,1)} %param.24) | copy-start | bytes 393220
  109.5 33.4 %copy-start.4 = (bf16[512,512]{1,0:T(8,128)(2,1)S(1)}, bf16[512,512]{1,0:T(8,128)(2,1)}, u32[]{:S(2)}) copy-start(bf16[512,512]{1,0:T(8,128)(2,1)} %param.18) | copy-start | bytes 1572868
  109.9 35.6 %copy-start.37 = (f32[512]{0:T(512)S(1)}, f32[512]{0:T(512)}, u32[]{:S(2)}) copy-start(f32[512]{0:T(512)} %param.20) | copy-start | bytes 6148
  110.8 36.0 %copy-start.30 = (bf16[512,32]{0,1:T(8,128)(2,1)S(1)}, bf16[512,32]{0,1:T(8,128)(2,1)}, u32[]{:S(2)}) copy-start(bf16[512,32]{0,1:T(8,128)(2,1)} %param.25) | copy-start | bytes 98308
  112.9 34.3 %copy-start.34 = (s32[16,32]{1,0:T(8,128)S(1)}, s32[16,32]{1,0:T(8,128)}, u32[]{:S(2)}) copy-start(s32[16,32]{1,0:T(8,128)} %param.30) | copy-start | bytes 6148
  112.9 66.5 %all-gather.7.cloned.1.call-start = ((), (), s32[]{:S(2)}) async-start(), calls=%async_computation.10 | async-start | bytes 2621440 | tf_op jit(solution)/shard_map/all_gather | solution.py:171
  146.8 182.2 %copy-start.5 = (bf16[512,512]{1,0:T(8,128)(2,1)}, bf16[512,512]{1,0:T(8,128)(2,1)S(1)}, u32[]{:S(2)}) copy-start(bf16[512,512]{1,0:T(8,128)(2,1)S(1)} %multiply_convert_fusion.3) | copy-start | bytes 1572868
  148.8 63.9 %all-gather.9.cloned.1.call-start = ((), (), s32[]{:S(2)}) async-start(), calls=%async_computation.12 | async-start | bytes 2621440 | tf_op jit(solution)/shard_map/all_gather | solution.py:201
  183.6 36.4 %all-to-all-start = ((bf16[32,64,512]{2,1,0:T(8,128)(2,1)}), bf16[32,64,512]{2,1,0:T(8,128)(2,1)}, u32[]{:S(2)}, u32[]{:S(2)}) async-start(bf16[32,64,512]{2,1,0:T(8,128)(2,1)} %copy.64), calls=%async_computation.1 | async-start | bytes 4194304 | tf_op jit(solution)/shard_map/all_to_all | solution.py:172
  220.0 33.7 %all-to-all-start.2 = ((bf16[32,64,512]{2,1,0:T(8,128)(2,1)}), bf16[32,64,512]{2,1,0:T(8,128)(2,1)}, u32[]{:S(2)}, u32[]{:S(2)}) async-start(bf16[32,64,512]{2,1,0:T(8,128)(2,1)} %copy.67), calls=%async_computation.4 | async-start | bytes 4194304 | tf_op jit(solution)/shard_map/all_to_all | solution.py:202
  225.2 103.8 %reduce-scatter.9.cloned.1.call-start = ((), (), s32[]{:S(2)}) async-start(), calls=%async_computation.13 | async-start | bytes 2621440 | tf_op jit(solution)/shard_map/reduce_scatter | solution.py:222
  293.9 61.5 %reduce-scatter.7.cloned.1.call-start = ((), (), s32[]{:S(2)}) async-start(), calls=%async_computation.11 | async-start | bytes 2621440 | tf_op jit(solution)/shard_map/reduce_scatter | solution.py:186
  296.8 58.6 %copy-start.10 = (bf16[512,512]{1,0:T(8,128)(2,1)S(1)}, bf16[512,512]{1,0:T(8,128)(2,1)}, u32[]{:S(2)}) copy-start(bf16[512,512]{1,0:T(8,128)(2,1)} %copy-done.9) | copy-start | bytes 1572868
  328.9 29.8 %copy-start.7 = (bf16[512,512]{1,0:T(8,128)(2,1)S(1)}, bf16[512,512]{1,0:T(8,128)(2,1)}, u32[]{:S(2)}) copy-start(bf16[512,512]{1,0:T(8,128)(2,1)} %reduce-scatter.5.cloned.1.call-done) | copy-start | bytes 1572868
  329.0 64.3 %all-gather.11.cloned.1.call-start = ((), (), s32[]{:S(2)}) async-start(), calls=%async_computation.14 | async-start | bytes 2621440 | tf_op jit(solution)/shard_map/all_gather | solution.py:242
  360.6 32.6 %copy-start.29 = (bf16[128,512]{1,0:T(8,128)(2,1)S(1)}, bf16[128,512]{1,0:T(8,128)(2,1)}, u32[]{:S(2)}) copy-start(bf16[128,512]{1,0:T(8,128)(2,1)} %param.24) | copy-start | bytes 393220
  362.5 141.8 %all-reduce.7.cloned.1.call-start = ((), (), s32[]{:S(2)}) async-start(), calls=%async_computation.16 | async-start | bytes 131072 | tf_op jit(solution)/shard_map/psum | solution.py:288
  363.5 230.1 %all-reduce.11.cloned.1.call-start = ((), (), s32[]{:S(2)}) async-start(), calls=%async_computation.18 | async-start | bytes 1048576 | tf_op jit(solution)/shard_map/psum | solution.py:282
  490.0 135.5 %reduce-scatter.11.cloned.1.call-start = ((), (), s32[]{:S(2)}) async-start(), calls=%async_computation.15 | async-start | bytes 2621440 | tf_op jit(solution)/shard_map/reduce_scatter | solution.py:270
  495.7 228.4 %all-reduce.9.cloned.1.call-start = ((), (), s32[]{:S(2)}) async-start(), calls=%async_computation.17 | async-start | bytes 131072 | tf_op jit(solution)/shard_map/psum | solution.py:287
  500.3 125.2 %copy-start.33 = (f32[512]{0:T(512)S(1)}, f32[512]{0:T(512)}, u32[]{:S(2)}) copy-start(f32[512]{0:T(512)} %copy-done.32) | copy-start | bytes 6148
  500.3 125.2 %copy-start.36 = (f32[512]{0:T(512)S(1)}, f32[512]{0:T(512)}, u32[]{:S(2)}) copy-start(f32[512]{0:T(512)} %copy-done.35) | copy-start | bytes 6148
  500.3 125.2 %copy-start.39 = (f32[512]{0:T(512)S(1)}, f32[512]{0:T(512)}, u32[]{:S(2)}) copy-start(f32[512]{0:T(512)} %param.19) | copy-start | bytes 6148
  500.4 126.9 %copy-start.14 = (f32[512,512]{1,0:T(8,128)S(1)}, f32[512,512]{1,0:T(8,128)}, u32[]{:S(2)}) copy-start(f32[512,512]{1,0:T(8,128)} %get-tuple-element.207) | copy-start | bytes 3145732
  500.4 225.2 %copy-start.1 = (bf16[1,512,512]{2,1,0:T(8,128)(2,1)S(1)}, bf16[1,512,512]{2,1,0:T(8,128)(2,1)}, u32[]{:S(2)}) copy-start(bf16[1,512,512]{2,1,0:T(8,128)(2,1)} %param.26) | copy-start | bytes 1572868
  (37 other events, 158.9 us)
Sparse Core Ops, SparseCore 0:
  12.1 34.2 all-gather.4
  113.1 29.8 reduce-scatter.4
  148.9 30.5 all-gather.6
  181.7 30.9 all-gather.8
  294.0 26.2 reduce-scatter.8
  329.1 26.2 reduce-scatter.6
  362.6 30.5 all-gather.10
  396.2 38.9 all-reduce.6
  490.2 103.4 all-reduce.10
  596.0 29.5 reduce-scatter.10
  628.8 95.1 all-reduce.8
